TPU v7x, 256 devices: a whole 4x4x8 slice. The times are simulated.
256 devices in a mesh: dp: 64 (over z, x, core), tensor: 4 (over y).
Axes of the slice: x: 4, y: 4, z: 8, core: 2. Of those that a mesh axis runs over, the one named last changes fastest.
Arguments:
- projections: bfloat16 [24576, 3, 3072], P('dp', None, 'tensor'), may hold values from -5.5 to 5.5
- routes: int32 [24576, 1], replicated, may hold values from 0 to 63; in each aligned block of 384 rows (0 to 383, 384 to 767, ...) at most 8 rows name the same one
- segments: int32 [64, 512], P('dp'), may hold values from 0 to 15, never falling along the last dimension, each value on 1 to 128 neighbouring positions
- out_weight: bfloat16 [3072, 6144], P('tensor'), may hold values from -0.109375 to 0.109375
Outputs:
- attention_out: bfloat16 [24576, 6144], P('dp', 'tensor')
Inputs may be any that keep to these rules, and one draw needn't show every extreme that they name: `routes`: at most 8 of the 384 rows of one device name the same sequence, and in every draw the rows of some device name some sequence exactly 8 times. `segments`: in each row the image numbers never fall, each image covers 1 to 128 positions, and one image covers exactly 128.
All inputs are finite; a program needn't handle non-finite values.
Results may differ from a plain program's by a relative error of at most 0.009.
Values may be sent and summed in bfloat16 or wider, within the bound.
No kernel may reach another device: no remote copies, remote signals or barrier semaphores. Data moves between devices by JAX's collectives and lax.ppermute only.
A program may use at most 64 MiB of HBM per device.

v0:
```python
import math

import jax
import jax.numpy as jnp
from jax import lax
from jax.sharding import PartitionSpec as P

HD = 128


def attend_heads(arrived, allowed):
    senders = arrived.shape[0]
    capacity = arrived.shape[1]
    slot_total = senders * capacity
    heads_now = arrived.shape[3]
    head_size = arrived.shape[4]
    flattened = arrived.reshape(slot_total, 3, heads_now, head_size)
    block_rows = min(slot_total, 512)
    block_count = slot_total // block_rows
    queries = flattened[:, 0].reshape(block_count, block_rows, heads_now, head_size)
    mask_rows = allowed.reshape(block_count, block_rows, slot_total)
    keys_in = flattened[:, 1]
    values_in = flattened[:, 2]
    scale = 1.0 / math.sqrt(head_size)

    def one_block(block_pair):
        query_block, mask_block = block_pair
        scores = (
            jnp.einsum("qhd,khd->hqk", query_block, keys_in, preferred_element_type=jnp.float32)
            * scale
        )
        scores = jnp.where(mask_block[None], scores, -jnp.inf)
        highest = jnp.max(scores, axis=2, keepdims=True)
        raised = jnp.exp(scores - highest)
        weights = (raised / jnp.sum(raised, axis=2, keepdims=True)).astype(jnp.bfloat16)
        return jnp.einsum(
            "hqk,khd->qhd", weights, values_in, preferred_element_type=jnp.float32
        ).astype(jnp.bfloat16)

    blocks = lax.map(one_block, (queries, mask_rows))
    return blocks.reshape(senders, capacity, heads_now, head_size)


def local(projections, routes, segments, out_weight):
    senders = lax.axis_size("dp")
    myself = lax.axis_index("dp")
    own_rows = projections.shape[0]
    column_count = projections.shape[2]
    heads_here = column_count // HD
    positions = segments.shape[1]
    capacity = positions // senders
    targets = routes[:, 0]
    my_routes = lax.dynamic_slice_in_dim(targets, myself * own_rows, own_rows)
    sequence_ids = jnp.arange(senders, dtype=jnp.int32)
    one_hot = (my_routes[:, None] == sequence_ids[None, :]).astype(jnp.int32)
    ranking = jnp.sum((jnp.cumsum(one_hot, axis=0) - one_hot) * one_hot, axis=1)
    slot_of_row = my_routes * capacity + ranking
    source_row = (
        jnp.zeros((positions,), jnp.int32)
        .at[slot_of_row]
        .set(jnp.arange(own_rows, dtype=jnp.int32))
    )
    outgoing = projections[source_row].reshape(senders, capacity, 3, heads_here, HD)
    arrivals = jnp.sum((targets.reshape(senders, own_rows) == myself).astype(jnp.int32), axis=1)
    earlier = jnp.cumsum(arrivals) - arrivals
    within = jnp.arange(capacity, dtype=jnp.int32)
    placed = earlier[:, None] + within[None, :]
    filled = within[None, :] < arrivals[:, None]
    flat_index = jnp.arange(positions, dtype=jnp.int32).reshape(senders, capacity)
    image_row = segments[0]
    looked_up = image_row[jnp.minimum(placed, positions - 1)]
    group_ids = jnp.where(filled, looked_up, -1 - flat_index).reshape(positions)
    allowed = group_ids[:, None] == group_ids[None, :]
    attended = attend_heads(
        lax.all_to_all(outgoing, "dp", split_axis=0, concat_axis=0, tiled=True), allowed
    )
    flat_heads = attended.reshape(positions, heads_here * HD)
    partial_value = jnp.dot(flat_heads, out_weight, preferred_element_type=jnp.float32)
    summed = lax.psum_scatter(
        partial_value.astype(jnp.bfloat16), "tensor", scatter_dimension=1, tiled=True
    )
    returned = lax.all_to_all(
        summed.reshape(senders, capacity, summed.shape[1]),
        "dp",
        split_axis=0,
        concat_axis=0,
        tiled=True,
    )
    result = returned.reshape(positions, returned.shape[2])[slot_of_row]
    return result


def solution(mesh):
    in_specs = (P("dp", None, "tensor"), P(), P("dp", None), P("tensor", None))
    out_specs = P("dp", "tensor")
    return jax.shard_map(local, mesh=mesh, in_specs=in_specs, out_specs=out_specs, check_vma=False)
```

profile of v0, /device:TPU:1, one launch (start us, length us, event | category | flops | bytes accessed | tf_op | source)
XLA Modules:
  0.0 232.9 jit_solution(11409188875466239145)
XLA Ops:
  6.5 0.0 copy-start
  6.5 0.8 dynamic-slice_reduce_fusion
  7.4 0.9 reduce-window.18
  8.3 0.2 slice_reduce_fusion
  8.6 0.1 fusion.11
  8.7 0.7 fusion.13
  9.4 2.9 %scatter_custom_fusion = s32[512]{0:T(512)S(1)} fusion(s32[384]{0:T(512)S(1)} %fusion.13, s32[384]{0:T(512)S(1)} %iota.32, s32[]{:T(128)} %constant.19.clone.1), kind=kCustom, calls=%fused_computation.41 | custom fusion | bytes 2052 | tf_op jit(solution)/shard_map/scatter | solution.py:61
  12.3 0.0 copy-done
  12.3 9.0 %gather_fusion = bf16[512,3,768]{2,0,1:T(8,128)(2,1)} fusion(bf16[384,3,768]{2,0,1:T(8,128)(2,1)S(1)} %copy-done, s32[1024]{0:T(1024)S(1)} %pad_clamp_fusion.2), kind=kCustom, calls=%fused_computation | custom fusion | bytes 4720640 | tf_op jit(solution)/shard_map/gather | solution.py:63
  21.4 0.0 copy-start.2
  21.4 0.0 copy-start.1
  21.4 3.5 %copy.15 = bf16[64,8,3,6,128]{4,1,3,2,0:T(8,128)(2,1)} copy(bf16[64,8,3,6,128]{4,1,3,0,2:T(8,128)(2,1)} %bitcast.47) | data formatting | bytes 4718592 | tf_op jit(solution)/shard_map/reshape | solution.py:63
  24.9 13.1 %all-to-all-start = ((bf16[64,8,3,6,128]{4,1,3,2,0:T(8,128)(2,1)}), bf16[64,8,3,6,128]{4,1,3,2,0:T(8,128)(2,1)}, u32[]{:S(2)}, u32[]{:S(2)}) async-start(bf16[64,8,3,6,128]{4,1,3,2,0:T(8,128)(2,1)} %copy.15), calls=%async_computation | async-start | bytes 4718592 | tf_op jit(solution)/shard_map/all_to_all | solution.py:75
  38.0 0.2 reduce-scatter.2.cloned.1.call-start
  38.3 0.0 copy-done.2
  38.3 0.3 fusion.8
  38.6 0.1 reduce_sum.32
  38.7 0.1 copy.17
  38.8 0.1 reduce-window.20
  38.9 0.1 reduce.5
  39.0 0.1 compare_select_fusion
  39.1 0.1 reshape.212
  39.2 0.0 copy-done.1
  39.2 3.5 %gather_fusion.1 = s32[512]{0:T(512)S(1)} fusion(s32[512]{0:T(512)S(1)} %bitcast.45, s32[1024]{0:T(1024)S(1)} %pad_clamp_fusion.1), kind=kCustom, calls=%fused_computation.1 | custom fusion | bytes 6144 | tf_op jit(solution)/shard_map/gather | solution.py:71
  42.7 0.1 reshape.211
  42.8 0.1 subtract_select_fusion
  42.9 0.1 select_n.46
  43.0 0.2 broadcast_compare_fusion
  43.2 50.1 %all-to-all-done = bf16[64,8,3,6,128]{4,1,3,2,0:T(8,128)(2,1)} async-done(((bf16[64,8,3,6,128]{4,1,3,2,0:T(8,128)(2,1)}), bf16[64,8,3,6,128]{4,1,3,2,0:T(8,128)(2,1)}, u32[]{:S(2)}, u32[]{:S(2)}) %all-to-all-start) | async-done | bytes 2359328 | tf_op jit(solution)/shard_map/all_to_all | solution.py:75
  93.3 2.3 copy.25
  95.6 1.0 fusion.7
  96.6 0.0 slice-start
  96.6 0.0 slice-start.1
  96.6 3.0 %fusion.18 = (f32[6,512]{1,0:T(8,128)S(1)}, f32[6,512,512]{1,2,0:T(8,128)S(1)}) fusion(f32[6,512,512]{1,2,0:T(8,128)S(1)} %fusion.7, pred[512,512]{0,1:T(8,128)(4,1)S(1)} %broadcast_compare_fusion), kind=kOutput, calls=%fused_computation.46 | output fusion | flops 9437695 | bytes 12857344 | tf_op jit(solution)/shard_map/while/body/eval_jaxpr/sub | solution.py:34
  99.6 0.0 slice-start.2
  99.7 0.8 fusion.6
  100.4 0.0 slice-done
  100.4 0.0 slice-done.1
  100.4 1.4 slice-done.2
  101.8 7.2 %convolution_convert_fusion = bf16[512,6144]{1,0:T(8,128)(2,1)} fusion(bf16[512,768]{0,1:T(8,128)(2,1)S(1)} %bitcast.56, bf16[768,6144]{1,0:T(8,128)(2,1)S(1)} %bitcast.55), kind=kOutput, calls=%fused_computation.5 | convolution fusion | flops 4834983936 | bytes 16515072 | tf_op jit(solution)/shard_map/dot_general | solution.py:78
  109.0 0.0 reduce-scatter.2.cloned.1.call-update
  109.1 64.4 %reduce-scatter.2.cloned.1.call-done = bf16[512,1536]{1,0:T(8,128)(2,1)} async-done(((bf16[512,6144]{1,0:T(8,128)(2,1)}), bf16[512,1536]{1,0:T(8,128)(2,1)}) %reduce-scatter.2.cloned.1.call-update) | async-done | bytes 1572880 | tf_op jit(solution)/shard_map/reduce_scatter | solution.py:79
  173.5 10.7 %all-to-all-start.1 = ((bf16[64,8,1536]{2,1,0:T(8,128)(2,1)}), bf16[64,8,1536]{2,1,0:T(8,128)(2,1)S(1)}, u32[]{:S(2)}, u32[]{:S(2)}) async-start(bf16[64,8,1536]{2,1,0:T(8,128)(2,1)} %bitcast.50), calls=%async_computation.2 | async-start | bytes 3145728 | tf_op jit(solution)/shard_map/all_to_all | solution.py:82
  184.2 39.0 %all-to-all-done.1 = bf16[64,8,1536]{2,1,0:T(8,128)(2,1)S(1)} async-done(((bf16[64,8,1536]{2,1,0:T(8,128)(2,1)}), bf16[64,8,1536]{2,1,0:T(8,128)(2,1)S(1)}, u32[]{:S(2)}, u32[]{:S(2)}) %all-to-all-start.1) | async-done | bytes 1572896 | tf_op jit(solution)/shard_map/all_to_all | solution.py:82
  223.2 2.8 %gather_fusion.2 = bf16[384,1536]{1,0:T(8,128)(2,1)} fusion(bf16[512,1536]{1,0:T(8,128)(2,1)S(1)} %bitcast.46, s32[1024]{0:T(1024)S(1)} %pad_clamp_fusion), kind=kCustom, calls=%fused_computation.2 | custom fusion | bytes 2360832 | tf_op jit(solution)/shard_map/gather | solution.py:89
  (10 shorter events, 0.1 us)
Async XLA Ops:
  6.5 5.8 %copy-start = (bf16[384,3,768]{2,0,1:T(8,128)(2,1)S(1)}, bf16[384,3,768]{2,0,1:T(8,128)(2,1)}, u32[]{:S(2)}) copy-start(bf16[384,3,768]{2,0,1:T(8,128)(2,1)} %param.4) | copy-start | bytes 5308420
  21.4 16.9 %copy-start.2 = (s32[24576,1]{0,1:T(1,128)S(1)}, s32[24576,1]{0,1:T(1,128)}, u32[]{:S(2)}) copy-start(s32[24576,1]{0,1:T(1,128)} %param.5) | copy-start | bytes 294916
  21.4 17.9 %copy-start.1 = (s32[1,512]{1,0:T(1,128)S(1)}, s32[1,512]{1,0:T(1,128)}, u32[]{:S(2)}) copy-start(s32[1,512]{1,0:T(1,128)} %param.6) | copy-start | bytes 6148
  24.9 68.4 %all-to-all-start = ((bf16[64,8,3,6,128]{4,1,3,2,0:T(8,128)(2,1)}), bf16[64,8,3,6,128]{4,1,3,2,0:T(8,128)(2,1)}, u32[]{:S(2)}, u32[]{:S(2)}) async-start(bf16[64,8,3,6,128]{4,1,3,2,0:T(8,128)(2,1)} %copy.15), calls=%async_computation | async-start | bytes 4718592 | tf_op jit(solution)/shard_map/all_to_all | solution.py:75
  38.0 135.4 %reduce-scatter.2.cloned.1.call-start = ((), (), s32[]{:S(2)}) async-start(), calls=%async_computation.3 | async-start | bytes 7864320 | tf_op jit(solution)/shard_map/reduce_scatter | solution.py:79
  96.6 3.8 %slice-start = ((s8[9437184]{0:T(1024)(128)(4,1)}), s8[1048576]{0:T(1024)(128)(4,1)S(1)}, s32[]{:S(2)}) async-start(s8[9437184]{0:T(1024)(128)(4,1)} %bitcast.54), calls=%async_computation.4 | async-start | bytes 2097152
  96.6 3.8 %slice-start.1 = ((s8[9437184]{0:T(1024)(128)(4,1)}), s8[4194304]{0:T(1024)(128)(4,1)S(1)}, s32[]{:S(2)}) async-start(s8[9437184]{0:T(1024)(128)(4,1)} %bitcast.54), calls=%async_computation.5 | async-start | bytes 8388608
  99.6 2.2 slice-start.2
  173.5 49.8 %all-to-all-start.1 = ((bf16[64,8,1536]{2,1,0:T(8,128)(2,1)}), bf16[64,8,1536]{2,1,0:T(8,128)(2,1)S(1)}, u32[]{:S(2)}, u32[]{:S(2)}) async-start(bf16[64,8,1536]{2,1,0:T(8,128)(2,1)} %bitcast.50), calls=%async_computation.2 | async-start | bytes 3145728 | tf_op jit(solution)/shard_map/all_to_all | solution.py:82
Sparse Core Ops, SparseCore 0:
  109.2 64.2 reduce-scatter.1
where the time goes:
time: 233 us
  waiting for transfers between devices  154 us (66%)
  local copies, waits for them, and re-layouts  26.9 us (12%)
  starting transfers between devices  24.1 us (10%)
  between operations  13.6 us (6%)
  matrix products  8.94 us (4%)
  other arithmetic  5.8 us (2%)
    reduce_scatter x1, waiting for transfers between devices, local(): lax.psum_scatter(partial_value.astype(jnp.bfloat16), 'tensor', scatter_di...  64.4 us
    all_to_all x1, waiting for transfers between devices, local(): lax.all_to_all(outgoing, 'dp', split_axis=0, concat_axis=0, tiled=True)  50.1 us
    all_to_all x1, waiting for transfers between devices, local(): lax.all_to_all(summed.reshape(senders, capacity, summed.shape[1]), 'dp',...  39 us
    all_to_all x1, starting transfers between devices, local(): lax.all_to_all(outgoing, 'dp', split_axis=0, concat_axis=0, tiled=True)  13.1 us
    all_to_all x1, starting transfers between devices, local(): lax.all_to_all(summed.reshape(senders, capacity, summed.shape[1]), 'dp',...  10.7 us
    gather x1, local copies, waits for them, and re-layouts, local(): projections[source_row].reshape(senders, capacity, 3, heads_here, HD)  9.01 us
    dot_general x1, matrix products, local(): jnp.dot(flat_heads, out_weight, preferred_element_type=jnp.float32)  7.2 us
  transfers between devices with their start and end apart: 3, of which 3 were waited for; matrix products, arithmetic and copies ran while one was open for 2% of the time, Pallas kernels for 0%

commit v1 on v0

v1 whole, which is shorter than its diff:
```python
import functools
import math

import jax
import jax.numpy as jnp
from jax import lax
from jax.experimental import pallas as pl
from jax.experimental.pallas import tpu as pltpu
from jax.sharding import PartitionSpec as P


HD = 128
VMEM = pltpu.MemorySpace.VMEM
HBM = pltpu.MemorySpace.HBM


def pack_kernel(capacity, rows_ref, data_ref, slot_ref, out_ref, held, built, in_sem, out_sem):
    own_rows = rows_ref.shape[1]
    positions = out_ref.shape[0]
    kinds, _, width = data_ref.shape
    senders = positions // capacity
    arriving = [
        pltpu.make_async_copy(data_ref.at[kind], held.at[kind], in_sem.at[kind])
        for kind in range(kinds)
    ]
    for copy in arriving:
        copy.start()
    routes = rows_ref[...]
    chosen = lax.broadcasted_iota(jnp.int32, (senders, own_rows), 0) == routes
    earlier = lax.broadcasted_iota(jnp.int32, (own_rows, own_rows), 0) < lax.broadcasted_iota(
        jnp.int32, (own_rows, own_rows), 1
    )
    counts = jnp.dot(
        chosen.astype(jnp.bfloat16),
        earlier.astype(jnp.bfloat16),
        preferred_element_type=jnp.float32,
    )
    ranking = jnp.sum(jnp.where(chosen, counts, 0.0), axis=0, keepdims=True).astype(jnp.int32)
    slots = routes * capacity + ranking
    slot_ref[...] = slots
    place = (lax.broadcasted_iota(jnp.int32, (positions, own_rows), 0) == slots).astype(
        jnp.bfloat16
    )
    leaving = []
    for kind in range(kinds):
        columns = slice(kind * width, (kind + 1) * width)
        arriving[kind].wait()
        built[:, columns] = jnp.dot(
            place, held[kind], preferred_element_type=jnp.float32
        ).astype(jnp.bfloat16)
        leaving.append(
            pltpu.make_async_copy(built.at[:, columns], out_ref.at[:, columns], out_sem.at[kind])
        )
        leaving[kind].start()
    for copy in leaving:
        copy.wait()


def pack(my_routes, by_kind, positions, capacity):
    kinds, own_rows, width = by_kind.shape
    return pl.pallas_call(
        functools.partial(pack_kernel, capacity),
        out_shape=(
            jax.ShapeDtypeStruct((1, own_rows), jnp.int32),
            jax.ShapeDtypeStruct((positions, kinds * width), jnp.bfloat16),
        ),
        in_specs=[pl.BlockSpec(memory_space=VMEM), pl.BlockSpec(memory_space=HBM)],
        out_specs=(pl.BlockSpec(memory_space=VMEM), pl.BlockSpec(memory_space=HBM)),
        scratch_shapes=[
            pltpu.VMEM(by_kind.shape, jnp.bfloat16),
            pltpu.VMEM((positions, kinds * width), jnp.bfloat16),
            pltpu.SemaphoreType.DMA((kinds,)),
            pltpu.SemaphoreType.DMA((kinds,)),
        ],
        name="pack_rows",
    )(my_routes.reshape(1, own_rows), by_kind)


def attend_kernel(heads, group_col_ref, group_row_ref, data_ref, out_ref):
    width = heads * HD
    allowed = group_col_ref[...] == group_row_ref[...]
    scale = 1.0 / math.sqrt(HD)
    for head in range(heads):
        low, high = head * HD, (head + 1) * HD
        queries = data_ref[:, low:high]
        keys_in = data_ref[:, width + low : width + high]
        values_in = data_ref[:, 2 * width + low : 2 * width + high]
        scores = lax.dot_general(
            queries, keys_in, (((1,), (1,)), ((), ())), preferred_element_type=jnp.float32
        )
        scores = jnp.where(allowed, scores * scale, -jnp.inf)
        highest = jnp.max(scores, axis=1, keepdims=True)
        raised = jnp.exp(scores - highest)
        total = jnp.sum(raised, axis=1, keepdims=True)
        mixed = jnp.dot(
            raised.astype(jnp.bfloat16), values_in, preferred_element_type=jnp.float32
        )
        out_ref[:, low:high] = (mixed / total).astype(jnp.bfloat16)


def attend(group_ids, arrived, heads):
    positions = arrived.shape[0]
    return pl.pallas_call(
        functools.partial(attend_kernel, heads),
        out_shape=jax.ShapeDtypeStruct((positions, heads * HD), jnp.bfloat16),
        in_specs=[pl.BlockSpec(memory_space=VMEM)] * 3,
        out_specs=pl.BlockSpec(memory_space=VMEM),
        compiler_params=pltpu.CompilerParams(vmem_limit_bytes=20 * 2**20),
        name="attend_rows",
    )(group_ids.reshape(positions, 1), group_ids.reshape(1, positions), arrived)


def local(projections, routes, segments, out_weight):
    senders = lax.axis_size("dp")
    groups = lax.axis_size("tensor")
    myself = lax.axis_index("dp")
    my_group = lax.axis_index("tensor")
    own_rows = projections.shape[0]
    column_count = projections.shape[2]
    heads_here = column_count // HD
    positions = segments.shape[1]
    capacity = positions // senders
    out_columns = out_weight.shape[1] // groups
    targets = routes[:, 0]
    my_routes = lax.dynamic_slice_in_dim(targets, myself * own_rows, own_rows)
    slots, outgoing = pack(my_routes, jnp.transpose(projections, (1, 0, 2)), positions, capacity)
    arrived = lax.all_to_all(
        outgoing.reshape(senders, capacity, 3 * column_count),
        "dp",
        split_axis=0,
        concat_axis=0,
        tiled=True,
    ).reshape(positions, 3 * column_count)

    arrivals = jnp.sum((targets.reshape(senders, own_rows) == myself).astype(jnp.int32), axis=1)
    earlier = jnp.cumsum(arrivals) - arrivals
    within = jnp.arange(capacity, dtype=jnp.int32)
    placed = earlier[:, None] + within[None, :]
    filled = within[None, :] < arrivals[:, None]
    flat_index = jnp.arange(positions, dtype=jnp.int32).reshape(senders, capacity)
    looked_up = segments[0][jnp.minimum(placed, positions - 1)]
    group_ids = jnp.where(filled, looked_up, -1 - flat_index).reshape(positions)
    restore = (
        slots.reshape(own_rows, 1) == jnp.arange(positions, dtype=jnp.int32)[None, :]
    ).astype(jnp.bfloat16)

    def shifted(value, step):
        return lax.ppermute(
            value, "tensor", [(here, (here + step) % groups) for here in range(groups)]
        )

    def weight_columns(step):
        at = lax.rem(my_group + step, groups) * out_columns
        return lax.dynamic_slice_in_dim(out_weight, at, out_columns, axis=1)

    weights = [weight_columns(0)]
    for step in range(1, groups):
        weights.append(shifted(weight_columns(step), step))

    attended = attend(group_ids, arrived, heads_here)
    returned = lax.all_to_all(
        attended.reshape(senders, capacity, column_count),
        "dp",
        split_axis=0,
        concat_axis=0,
        tiled=True,
    ).reshape(positions, column_count)
    mine = jnp.dot(restore, returned, preferred_element_type=jnp.float32).astype(jnp.bfloat16)
    pieces = [mine]
    for step in range(1, groups):
        pieces.append(shifted(mine, step))
    total = jnp.dot(pieces[0], weights[0], preferred_element_type=jnp.float32)
    for step in (1, 3, 2):
        total = total + jnp.dot(pieces[step], weights[step], preferred_element_type=jnp.float32)
    return total.astype(jnp.bfloat16)


def solution(mesh):
    in_specs = (P("dp", None, "tensor"), P(), P("dp", None), P("tensor", None))
    out_specs = P("dp", "tensor")
    return jax.shard_map(local, mesh=mesh, in_specs=in_specs, out_specs=out_specs, check_vma=False)
```

time: 233 us -> 229 us (0.983)
  local copies, waits for them, and re-layouts: 26.9 us -> 11 us
  between operations: 13.6 us -> 0.21 us
  Pallas kernels: 0 us -> 9.11 us
  waiting for transfers between devices: 154 us -> 162 us
  starting transfers between devices: 24.1 us -> 31.7 us
  other arithmetic: 5.8 us -> 0.79 us
  matrix products: 8.94 us -> 13.5 us
    ppermute x0 -> x6, waiting for transfers between devices: none -> 100 us  [shifted(): lax.ppermute(value, 'tensor', [(here, (here + step) % groups) for here in...]
    reduce_scatter x1 -> x0, waiting for transfers between devices: 64.4 us -> none  [local(): lax.psum_scatter(partial_value.astype(jnp.bfloat16), 'tensor', scatter_di...]
    all_to_all x2, waiting for transfers between devices: 89.2 us -> 62.1 us  [the longest x1 50.4 us: local(): lax.all_to_all(outgoing.reshape(senders, capacity, 3 * column_count), 'dp...]
    gather x4 -> x2, local copies, waits for them, and re-layouts: 15.4 us -> 3.6 us  [local(): looked_up = segments[0][jnp.minimum(placed, positions - 1)]]
    ppermute x0 -> x6, starting transfers between devices: none -> 11.7 us  [shifted(): lax.ppermute(value, 'tensor', [(here, (here + step) % groups) for here in...]
    pallas_call x0 -> x2, Pallas kernels: none -> 9.11 us  [the longest x1 5.34 us: pack(): pl.pallas_call(functools.partial(pack_kernel, capacity), out_shape=(jax.S...]
    dynamic_slice x1, local copies, waits for them, and re-layouts: 0.83 us -> 5.69 us  [weight_columns(): return lax.dynamic_slice_in_dim(out_weight, at, out_columns, axis=1)]
    dot_general x3 -> x5, matrix products: 8.94 us -> 13.5 us  [the longest x3 9.27 us: local(): jnp.dot(pieces[step], weights[step], preferred_element_type=jnp.float32)]
  transfers between devices with their start and end apart: 3 -> 8, of which waited for: 3 -> 5; matrix products, arithmetic and copies ran while one was open for 2% -> 9% of each run, Pallas kernels for 0% -> 0%
where the time goes in v1:
time: 229 us
  waiting for transfers between devices  162 us (71%)
  starting transfers between devices  31.7 us (14%)
  matrix products  13.5 us (6%)
  local copies, waits for them, and re-layouts  11 us (5%)
  Pallas kernels  9.11 us (4%)
    ppermute x6, waiting for transfers between devices, shifted(): lax.ppermute(value, 'tensor', [(here, (here + step) % groups) for here in...  100 us
    all_to_all x1, waiting for transfers between devices, local(): lax.all_to_all(outgoing.reshape(senders, capacity, 3 * column_count), 'dp...  50.4 us
    all_to_all x1, starting transfers between devices, local(): lax.all_to_all(outgoing.reshape(senders, capacity, 3 * column_count), 'dp...  13.1 us
    all_to_all x1, waiting for transfers between devices, local(): lax.all_to_all(attended.reshape(senders, capacity, column_count), 'dp', s...  11.7 us
    ppermute x6, starting transfers between devices, shifted(): lax.ppermute(value, 'tensor', [(here, (here + step) % groups) for here in...  11.7 us
    dot_general x3, matrix products, local(): jnp.dot(pieces[step], weights[step], preferred_element_type=jnp.float32)  9.27 us
    all_to_all x1, starting transfers between devices, local(): lax.all_to_all(attended.reshape(senders, capacity, column_count), 'dp', s...  6.93 us
    dynamic_slice x1, local copies, waits for them, and re-layouts, weight_columns(): return lax.dynamic_slice_in_dim(out_weight, at, out_columns, axis=1)  5.69 us
  transfers between devices with their start and end apart: 8, of which 5 were waited for; matrix products, arithmetic and copies ran while one was open for 9% of the time, Pallas kernels for 0%

profile of v1, /device:TPU:1, one launch (start us, length us, event | category | flops | bytes accessed | tf_op | source)
XLA Modules:
  0.0 228.8 jit_solution(8621218267835243039)
XLA Ops:
  0.0 0.0 copy-start
  0.0 1.3 dynamic-slice_bitcast_fusion.rows_ref
  1.3 5.3 %pack_rows.1 = (s32[1,384]{1,0:T(1,128)}, bf16[512,2304]{1,0:T(8,128)(2,1)}) custom-call(s32[1,384]{1,0:T(1,128)} %dynamic-slice_bitcast_fusion.rows_ref, bf16[3,384,768]{2,1,0:T(8,128)(2,1)} %bitcast.23), custom_call_target="tpu_custom_call" | custom-call | tf_op jit(solution)/shard_map/pack_rows/pallas_call | solution.py:61
  6.6 0.0 copy-start.1
  6.6 13.1 %all-to-all-start = ((bf16[64,8,2304]{2,1,0:T(8,128)(2,1)}), bf16[64,8,2304]{2,1,0:T(8,128)(2,1)S(1)}, u32[]{:S(2)}, u32[]{:S(2)}) async-start(bf16[64,8,2304]{2,1,0:T(8,128)(2,1)} %bitcast.22), calls=%async_computation | async-start | bytes 4718592 | tf_op jit(solution)/shard_map/all_to_all | solution.py:127
  19.8 0.0 copy-done.1
  19.8 0.3 fusion.6
  20.1 0.1 reduce_sum.9
  20.2 0.1 copy.6
  20.3 0.1 reduce-window.8
  20.4 0.1 reduce.2
  20.5 0.1 compare_select_fusion
  20.6 0.1 reshape.242
  20.7 0.0 copy-done
  20.7 3.5 %gather_fusion = s32[512]{0:T(512)S(1)} fusion(s32[512]{0:T(512)S(1)} %bitcast.20, s32[1024]{0:T(1024)S(1)} %pad_clamp_fusion), kind=kCustom, calls=%fused_computation | custom fusion | bytes 6144 | tf_op jit(solution)/shard_map/gather | solution.py:141
  24.3 0.1 reshape.241
  24.3 0.1 subtract_select_fusion
  24.4 0.1 select_n.58.group_col_ref
  24.6 0.1 select_n.53.group_row_ref
  24.7 50.4 %all-to-all-done = bf16[64,8,2304]{2,1,0:T(8,128)(2,1)S(1)} async-done(((bf16[64,8,2304]{2,1,0:T(8,128)(2,1)}), bf16[64,8,2304]{2,1,0:T(8,128)(2,1)S(1)}, u32[]{:S(2)}, u32[]{:S(2)}) %all-to-all-start) | async-done | bytes 2359328 | tf_op jit(solution)/shard_map/all_to_all | solution.py:127
  75.1 3.8 %attend_rows.1 = bf16[512,768]{1,0:T(8,128)(2,1)} custom-call(s32[512,1]{1,0:T(8,128)S(1)} %select_n.58.group_col_ref, s32[1,512]{1,0:T(1,128)S(1)} %select_n.53.group_row_ref, bf16[512,2304]{1,0:T(8,128)(2,1)S(1)} %bitcast.21), custom_call_target="tpu_custom_call" | custom-call | tf_op jit(solution)/shard_map/attend_rows/pallas_call | solution.py:103
  78.9 6.9 %all-to-all-start.1 = ((bf16[64,8,768]{2,1,0:T(8,128)(2,1)}), bf16[64,8,768]{2,1,0:T(8,128)(2,1)S(1)}, u32[]{:S(2)}, u32[]{:S(2)}) async-start(bf16[64,8,768]{2,1,0:T(8,128)(2,1)} %bitcast.6), calls=%async_computation.1 | async-start | bytes 1572864 | tf_op jit(solution)/shard_map/all_to_all | solution.py:161
  85.8 0.0 copy-start.2
  85.8 5.7 %constant_dynamic-slice_fusion.1 = (bf16[768,1536]{1,0:T(8,128)(2,1)S(1)}, bf16[768,1536]{1,0:T(8,128)(2,1)}, bf16[768,1536]{1,0:T(8,128)(2,1)}) fusion(bf16[768,6144]{1,0:T(8,128)(2,1)} %param.7, s32[]{:T(128)S(6)} %select_n.56, s32[]{:T(128)S(6)} %select_n.55, s32[]{:T(128)S(6)} %select_n.57), kind=kLoop, calls=%fused_computation.19 | loop fusion | bytes 14155788 | tf_op jit(solution)/shard_map/dynamic_slice | solution.py:154
  91.5 2.9 %collective-permute-start.5 = (bf16[768,1536]{1,0:T(8,128)(2,1)}, bf16[768,1536]{1,0:T(8,128)(2,1)}, u32[]{:S(2)}, u32[]{:S(2)}) collective-permute-start(bf16[768,1536]{1,0:T(8,128)(2,1)} %get-tuple-element.11), channel_id=1, source_target_pairs={{0,2},{1,3},{2,0},{3,1},{4,6},{5,7},{6,4},{7,5},{8,10},{9,11},{10,... | collective-permute-start | bytes 7077896 | tf_op jit(solution)/shard_map/ppermute | solution.py:148
  94.4 0.4 collective-permute-start.1
  94.8 2.3 collective-permute-start.3
  97.1 0.0 copy-done.2
  97.1 11.7 %all-to-all-done.1 = bf16[64,8,768]{2,1,0:T(8,128)(2,1)S(1)} async-done(((bf16[64,8,768]{2,1,0:T(8,128)(2,1)}), bf16[64,8,768]{2,1,0:T(8,128)(2,1)S(1)}, u32[]{:S(2)}, u32[]{:S(2)}) %all-to-all-start.1) | async-done | bytes 786464 | tf_op jit(solution)/shard_map/all_to_all | solution.py:161
  108.8 1.3 convolution_convert_fusion
  110.1 2.9 %collective-permute-start.4 = (bf16[384,768]{1,0:T(8,128)(2,1)}, bf16[384,768]{1,0:T(8,128)(2,1)S(1)}, u32[]{:S(2)}, u32[]{:S(2)}) collective-permute-start(bf16[384,768]{1,0:T(8,128)(2,1)} %convolution_convert_fusion), channel_id=1, source_target_pairs={{0,2},{1,3},{2,0},{3,1},{4,6},{5,7},{6,4},{7,5},{8,10},{9,11},{10,... | collective-permute-start | bytes 1769480 | tf_op jit(solution)/shard_map/ppermute | solution.py:148
  113.1 0.4 collective-permute-start
  113.5 2.9 %fusion.2 = f32[384,1536]{1,0:T(8,128)S(1)} fusion(bf16[384,768]{1,0:T(8,128)(2,1)} %convolution_convert_fusion, bf16[768,6144]{1,0:T(8,128)(2,1)} %param.7, s32[]{:T(128)S(6)} %select_n.54), kind=kOutput, calls=%fused_computation.5 | convolution fusion | flops 905969664 | bytes 5308420 | tf_op jit(solution)/shard_map/dot_general | solution.py:172
  116.4 29.3 %collective-permute-done.5 = bf16[768,1536]{1,0:T(8,128)(2,1)} collective-permute-done((bf16[768,1536]{1,0:T(8,128)(2,1)}, bf16[768,1536]{1,0:T(8,128)(2,1)}, u32[]{:S(2)}, u32[]{:S(2)}) %collective-permute-start.5) | collective-permute-done | bytes 2359328 | tf_op jit(solution)/shard_map/ppermute | solution.py:148
  145.7 2.7 %collective-permute-start.2 = (bf16[384,768]{1,0:T(8,128)(2,1)}, bf16[384,768]{1,0:T(8,128)(2,1)S(1)}, u32[]{:S(2)}, u32[]{:S(2)}) collective-permute-start(bf16[384,768]{1,0:T(8,128)(2,1)} %convolution_convert_fusion), channel_id=1, source_target_pairs={{0,3},{1,0},{2,1},{3,2},{4,7},{5,4},{6,5},{7,6},{8,11},{9,8},{10,9... | collective-permute-start | bytes 1769480 | tf_op jit(solution)/shard_map/ppermute | solution.py:148
  148.5 60.4 %collective-permute-done.4 = bf16[384,768]{1,0:T(8,128)(2,1)S(1)} collective-permute-done((bf16[384,768]{1,0:T(8,128)(2,1)}, bf16[384,768]{1,0:T(8,128)(2,1)S(1)}, u32[]{:S(2)}, u32[]{:S(2)}) %collective-permute-start.4) | collective-permute-done | bytes 589856 | tf_op jit(solution)/shard_map/ppermute | solution.py:148
  208.9 2.7 %fusion.8 = f32[384,1536]{1,0:T(8,128)S(1)} fusion(bf16[384,768]{1,0:T(8,128)(2,1)S(1)} %collective-permute-done.4, bf16[768,1536]{1,0:T(8,128)(2,1)} %collective-permute-done.5), kind=kOutput, calls=%fused_computation.22 | convolution fusion | flops 905969664 | bytes 5308416 | tf_op jit(solution)/shard_map/dot_general | solution.py:174
  211.6 0.0 collective-permute-done.1
  211.6 10.6 %collective-permute-done = bf16[384,768]{1,0:T(8,128)(2,1)S(1)} collective-permute-done((bf16[384,768]{1,0:T(8,128)(2,1)}, bf16[384,768]{1,0:T(8,128)(2,1)S(1)}, u32[]{:S(2)}, u32[]{:S(2)}) %collective-permute-start) | collective-permute-done | bytes 589856 | tf_op jit(solution)/shard_map/ppermute | solution.py:148
  222.2 2.7 %convolution_add_fusion.1 = f32[384,1536]{1,0:T(8,128)S(1)} fusion(f32[384,1536]{1,0:T(8,128)S(1)} %fusion.2, bf16[384,768]{1,0:T(8,128)(2,1)S(1)} %collective-permute-done, bf16[768,1536]{1,0:T(8,128)(2,1)} %collective-permute-done.1), kind=kOutput, calls=%fused_computation.2 | convolution fusion | flops 906559488 | bytes 7667712 | tf_op jit(solution)/shard_map/dot_general | solution.py:174
  225.0 0.0 collective-permute-done.3
  225.0 0.0 collective-permute-done.2
  225.0 3.8 %fusion.1 = bf16[384,1536]{1,0:T(8,128)(2,1)} fusion(f32[384,1536]{1,0:T(8,128)S(1)} %fusion.8, f32[384,1536]{1,0:T(8,128)S(1)} %convolution_add_fusion.1, bf16[384,768]{1,0:T(8,128)(2,1)S(1)} %collective-permute-done.2, bf16[768,1536]{1,0:T(8,128)(2,1)} %collective-permute-done.3), kind=kOutput, calls=%fused_computation.4 | convolution fusion | flops 907739136 | bytes 8847360 | tf_op jit(solution)/shard_map/dot_general | solution.py:174
  (4 shorter events, 0.1 us)
Async XLA Ops:
  0.0 20.7 %copy-start = (s32[1,512]{1,0:T(1,128)S(1)}, s32[1,512]{1,0:T(1,128)}, u32[]{:S(2)}) copy-start(s32[1,512]{1,0:T(1,128)} %param.6) | copy-start | bytes 6148
  6.6 13.2 %copy-start.1 = (s32[24576,1]{0,1:T(1,128)S(1)}, s32[24576,1]{0,1:T(1,128)}, u32[]{:S(2)}) copy-start(s32[24576,1]{0,1:T(1,128)} %param.5) | copy-start | bytes 294916
  6.6 68.5 %all-to-all-start = ((bf16[64,8,2304]{2,1,0:T(8,128)(2,1)}), bf16[64,8,2304]{2,1,0:T(8,128)(2,1)S(1)}, u32[]{:S(2)}, u32[]{:S(2)}) async-start(bf16[64,8,2304]{2,1,0:T(8,128)(2,1)} %bitcast.22), calls=%async_computation | async-start | bytes 4718592 | tf_op jit(solution)/shard_map/all_to_all | solution.py:127
  78.9 29.9 %all-to-all-start.1 = ((bf16[64,8,768]{2,1,0:T(8,128)(2,1)}), bf16[64,8,768]{2,1,0:T(8,128)(2,1)S(1)}, u32[]{:S(2)}, u32[]{:S(2)}) async-start(bf16[64,8,768]{2,1,0:T(8,128)(2,1)} %bitcast.6), calls=%async_computation.1 | async-start | bytes 1572864 | tf_op jit(solution)/shard_map/all_to_all | solution.py:161
  85.8 11.3 %copy-start.2 = (s32[1,384]{1,0:T(1,128)S(1)}, s32[1,384]{1,0:T(1,128)}, u32[]{:S(2)}) copy-start(s32[1,384]{1,0:T(1,128)} %get-tuple-element.7) | copy-start | bytes 4612
  91.5 54.2 %collective-permute-start.5 = (bf16[768,1536]{1,0:T(8,128)(2,1)}, bf16[768,1536]{1,0:T(8,128)(2,1)}, u32[]{:S(2)}, u32[]{:S(2)}) collective-permute-start(bf16[768,1536]{1,0:T(8,128)(2,1)} %get-tuple-element.11), channel_id=1, source_target_pairs={{0,2},{1,3},{2,0},{3,1},{4,6},{5,7},{6,4},{7,5},{8,10},{9,11},{10,... | collective-permute-start | bytes 7077896 | tf_op jit(solution)/shard_map/ppermute | solution.py:148
  94.4 117.2 %collective-permute-start.1 = (bf16[768,1536]{1,0:T(8,128)(2,1)}, bf16[768,1536]{1,0:T(8,128)(2,1)}, u32[]{:S(2)}, u32[]{:S(2)}) collective-permute-start(bf16[768,1536]{1,0:T(8,128)(2,1)} %get-tuple-element.10), channel_id=1, source_target_pairs={{0,1},{1,2},{2,3},{3,0},{4,5},{5,6},{6,7},{7,4},{8,9},{9,10},{10,1... | collective-permute-start | bytes 7077896 | tf_op jit(solution)/shard_map/ppermute | solution.py:148
  94.8 130.2 %collective-permute-start.3 = (bf16[768,1536]{1,0:T(8,128)(2,1)S(1)}, bf16[768,1536]{1,0:T(8,128)(2,1)}, u32[]{:S(2)}, u32[]{:S(2)}) collective-permute-start(bf16[768,1536]{1,0:T(8,128)(2,1)S(1)} %get-tuple-element.9), channel_id=1, source_target_pairs={{0,3},{1,0},{2,1},{3,2},{4,7},{5,4},{6,5},{7,6},{8,11},{9,8},{10,9... | collective-permute-start | bytes 7077896 | tf_op jit(solution)/shard_map/ppermute | solution.py:148
  110.1 98.7 %collective-permute-start.4 = (bf16[384,768]{1,0:T(8,128)(2,1)}, bf16[384,768]{1,0:T(8,128)(2,1)S(1)}, u32[]{:S(2)}, u32[]{:S(2)}) collective-permute-start(bf16[384,768]{1,0:T(8,128)(2,1)} %convolution_convert_fusion), channel_id=1, source_target_pairs={{0,2},{1,3},{2,0},{3,1},{4,6},{5,7},{6,4},{7,5},{8,10},{9,11},{10,... | collective-permute-start | bytes 1769480 | tf_op jit(solution)/shard_map/ppermute | solution.py:148
  113.1 109.2 %collective-permute-start = (bf16[384,768]{1,0:T(8,128)(2,1)}, bf16[384,768]{1,0:T(8,128)(2,1)S(1)}, u32[]{:S(2)}, u32[]{:S(2)}) collective-permute-start(bf16[384,768]{1,0:T(8,128)(2,1)} %convolution_convert_fusion), channel_id=1, source_target_pairs={{0,1},{1,2},{2,3},{3,0},{4,5},{5,6},{6,7},{7,4},{8,9},{9,10},{10,1... | collective-permute-start | bytes 1769480 | tf_op jit(solution)/shard_map/ppermute | solution.py:148
  145.7 79.3 %collective-permute-start.2 = (bf16[384,768]{1,0:T(8,128)(2,1)}, bf16[384,768]{1,0:T(8,128)(2,1)S(1)}, u32[]{:S(2)}, u32[]{:S(2)}) collective-permute-start(bf16[384,768]{1,0:T(8,128)(2,1)} %convolution_convert_fusion), channel_id=1, source_target_pairs={{0,3},{1,0},{2,1},{3,2},{4,7},{5,4},{6,5},{7,6},{8,11},{9,8},{10,9... | collective-permute-start | bytes 1769480 | tf_op jit(solution)/shard_map/ppermute | solution.py:148

commit v2 on v1

--- a/solution.py
+++ b/solution.py
@@ -14,8 +14,10 @@
 HBM = pltpu.MemorySpace.HBM
 
 
-def pack_kernel(capacity, rows_ref, data_ref, slot_ref, out_ref, held, built, in_sem, out_sem):
-    own_rows = rows_ref.shape[1]
+def pack_kernel(
+    capacity, routes_ref, data_ref, slot_ref, out_ref, named, held, built, in_sem, out_sem
+):
+    own_rows = named.shape[1]
     positions = out_ref.shape[0]
     kinds, _, width = data_ref.shape
     senders = positions // capacity
@@ -23,9 +25,15 @@
         pltpu.make_async_copy(data_ref.at[kind], held.at[kind], in_sem.at[kind])
         for kind in range(kinds)
     ]
+    own_at = pl.multiple_of(lax.axis_index("dp") * own_rows, own_rows)
+    naming = pltpu.make_async_copy(
+        routes_ref.at[:, pl.ds(own_at, own_rows)], named, in_sem.at[kinds]
+    )
+    naming.start()
     for copy in arriving:
         copy.start()
-    routes = rows_ref[...]
+    naming.wait()
+    routes = named[...]
     chosen = lax.broadcasted_iota(jnp.int32, (senders, own_rows), 0) == routes
     earlier = lax.broadcasted_iota(jnp.int32, (own_rows, own_rows), 0) < lax.broadcasted_iota(
         jnp.int32, (own_rows, own_rows), 1
@@ -56,7 +64,7 @@
         copy.wait()
 
 
-def pack(my_routes, by_kind, positions, capacity):
+def pack(routes, by_kind, positions, capacity):
     kinds, own_rows, width = by_kind.shape
     return pl.pallas_call(
         functools.partial(pack_kernel, capacity),
@@ -64,27 +72,45 @@
             jax.ShapeDtypeStruct((1, own_rows), jnp.int32),
             jax.ShapeDtypeStruct((positions, kinds * width), jnp.bfloat16),
         ),
-        in_specs=[pl.BlockSpec(memory_space=VMEM), pl.BlockSpec(memory_space=HBM)],
+        in_specs=[pl.BlockSpec(memory_space=HBM)] * 2,
         out_specs=(pl.BlockSpec(memory_space=VMEM), pl.BlockSpec(memory_space=HBM)),
         scratch_shapes=[
+            pltpu.VMEM((1, own_rows), jnp.int32),
             pltpu.VMEM(by_kind.shape, jnp.bfloat16),
             pltpu.VMEM((positions, kinds * width), jnp.bfloat16),
-            pltpu.SemaphoreType.DMA((kinds,)),
+            pltpu.SemaphoreType.DMA((kinds + 1,)),
             pltpu.SemaphoreType.DMA((kinds,)),
         ],
         name="pack_rows",
-    )(my_routes.reshape(1, own_rows), by_kind)
-
-
-def attend_kernel(heads, group_col_ref, group_row_ref, data_ref, out_ref):
+    )(routes, by_kind)
+
+
+def attend_kernel(
+    heads, group_col_ref, group_row_ref, data_ref, out_ref, held, built, in_sem, out_sem
+):
     width = heads * HD
+    arriving, leaving = [], []
+    for head in range(heads):
+        parts = []
+        for kind in range(3):
+            low = kind * width + head * HD
+            columns = slice(low, low + HD)
+            parts.append(
+                pltpu.make_async_copy(
+                    data_ref.at[:, columns], held.at[:, columns], in_sem.at[3 * head + kind]
+                )
+            )
+            parts[kind].start()
+        arriving.append(parts)
     allowed = group_col_ref[...] == group_row_ref[...]
     scale = 1.0 / math.sqrt(HD)
     for head in range(heads):
         low, high = head * HD, (head + 1) * HD
-        queries = data_ref[:, low:high]
-        keys_in = data_ref[:, width + low : width + high]
-        values_in = data_ref[:, 2 * width + low : 2 * width + high]
+        for copy in arriving[head]:
+            copy.wait()
+        queries = held[:, low:high]
+        keys_in = held[:, width + low : width + high]
+        values_in = held[:, 2 * width + low : 2 * width + high]
         scores = lax.dot_general(
             queries, keys_in, (((1,), (1,)), ((), ())), preferred_element_type=jnp.float32
         )
@@ -95,19 +121,99 @@
         mixed = jnp.dot(
             raised.astype(jnp.bfloat16), values_in, preferred_element_type=jnp.float32
         )
-        out_ref[:, low:high] = (mixed / total).astype(jnp.bfloat16)
+        built[:, low:high] = (mixed / total).astype(jnp.bfloat16)
+        leaving.append(
+            pltpu.make_async_copy(
+                built.at[:, low:high], out_ref.at[:, low:high], out_sem.at[head]
+            )
+        )
+        leaving[head].start()
+    for copy in leaving:
+        copy.wait()
 
 
 def attend(group_ids, arrived, heads):
     positions = arrived.shape[0]
+    shape = (positions, heads * HD)
     return pl.pallas_call(
         functools.partial(attend_kernel, heads),
-        out_shape=jax.ShapeDtypeStruct((positions, heads * HD), jnp.bfloat16),
-        in_specs=[pl.BlockSpec(memory_space=VMEM)] * 3,
-        out_specs=pl.BlockSpec(memory_space=VMEM),
-        compiler_params=pltpu.CompilerParams(vmem_limit_bytes=20 * 2**20),
+        out_shape=jax.ShapeDtypeStruct(shape, jnp.bfloat16),
+        in_specs=[pl.BlockSpec(memory_space=VMEM)] * 2 + [pl.BlockSpec(memory_space=HBM)],
+        out_specs=pl.BlockSpec(memory_space=HBM),
+        scratch_shapes=[
+            pltpu.VMEM(arrived.shape, jnp.bfloat16),
+            pltpu.VMEM(shape, jnp.bfloat16),
+            pltpu.SemaphoreType.DMA((3 * heads,)),
+            pltpu.SemaphoreType.DMA((heads,)),
+        ],
         name="attend_rows",
     )(group_ids.reshape(positions, 1), group_ids.reshape(1, positions), arrived)
+
+
+def restore_kernel(at_ref, place_ref, data_ref, first_ref, second_ref):
+    half = first_ref.shape[1]
+    for at, out_ref in ((at_ref[0], first_ref), (half - at_ref[0], second_ref)):
+        columns = data_ref[:, pl.ds(pl.multiple_of(at, half), half)]
+        out_ref[...] = jnp.dot(
+            place_ref[...], columns, preferred_element_type=jnp.float32
+        ).astype(jnp.bfloat16)
+
+
+def restored(first_at, place, data):
+    shape = jax.ShapeDtypeStruct((place.shape[0], data.shape[1] // 2), jnp.bfloat16)
+    return pl.pallas_call(
+        restore_kernel,
+        out_shape=(shape, shape),
+        in_specs=[pl.BlockSpec(memory_space=pltpu.MemorySpace.SMEM)]
+        + [pl.BlockSpec(memory_space=VMEM)] * 2,
+        out_specs=(pl.BlockSpec(memory_space=VMEM),) * 2,
+        compiler_params=pltpu.CompilerParams(vmem_limit_bytes=20 * 2**20),
+        name="restore_rows",
+    )(first_at.reshape(1), place, data)
+
+
+def mix_kernel(count, has_total, *refs):
+    rows, weights = refs[:count], refs[count : 2 * count]
+    out_ref = refs[2 * count + has_total]
+    width = out_ref.shape[1]
+    step = 512
+    staged = refs[2 * count + has_total + 1 :]
+    copies = []
+    for at, low in enumerate(range(0, width, step)):
+        columns = slice(low, low + step)
+        total = refs[2 * count][:, columns] if has_total else None
+        for row, weight in zip(rows, weights):
+            term = jnp.dot(row[...], weight[:, columns], preferred_element_type=jnp.float32)
+            total = term if total is None else total + term
+        if staged:
+            staged[0][:, columns] = total.astype(staged[0].dtype)
+            copies.append(
+                pltpu.make_async_copy(
+                    staged[0].at[:, columns], out_ref.at[:, columns], staged[1].at[at]
+                )
+            )
+            copies[at].start()
+        else:
+            out_ref[:, columns] = total
+    for copy in copies:
+        copy.wait()
+
+
+def mix(rows, weights, total=None, last=False):
+    shape = (rows[0].shape[0], weights[0].shape[1])
+    given = [*rows, *weights] + ([] if total is None else [total])
+    dtype = jnp.bfloat16 if last else jnp.float32
+    return pl.pallas_call(
+        functools.partial(mix_kernel, len(rows), total is not None),
+        out_shape=jax.ShapeDtypeStruct(shape, dtype),
+        in_specs=[pl.BlockSpec(memory_space=VMEM)] * len(given),
+        out_specs=pl.BlockSpec(memory_space=HBM if last else VMEM),
+        scratch_shapes=(
+            [pltpu.VMEM(shape, dtype), pltpu.SemaphoreType.DMA((shape[1] // 512,))] if last else []
+        ),
+        compiler_params=pltpu.CompilerParams(vmem_limit_bytes=20 * 2**20),
+        name="mix_last" if last else "mix_some",
+    )(*given)
 
 
 def local(projections, routes, segments, out_weight):
@@ -121,9 +227,16 @@
     positions = segments.shape[1]
     capacity = positions // senders
     out_columns = out_weight.shape[1] // groups
+    half = column_count // 2
+    first_at = (myself % 2) * half
+    second_at = half - first_at
     targets = routes[:, 0]
-    my_routes = lax.dynamic_slice_in_dim(targets, myself * own_rows, own_rows)
-    slots, outgoing = pack(my_routes, jnp.transpose(projections, (1, 0, 2)), positions, capacity)
+    slots, outgoing = pack(
+        targets.reshape(1, senders * own_rows),
+        jnp.transpose(projections, (1, 0, 2)),
+        positions,
+        capacity,
+    )
     arrived = lax.all_to_all(
         outgoing.reshape(senders, capacity, 3 * column_count),
         "dp",
@@ -149,13 +262,16 @@
             value, "tensor", [(here, (here + step) % groups) for here in range(groups)]
         )
 
-    def weight_columns(step):
-        at = lax.rem(my_group + step, groups) * out_columns
-        return lax.dynamic_slice_in_dim(out_weight, at, out_columns, axis=1)
-
-    weights = [weight_columns(0)]
-    for step in range(1, groups):
-        weights.append(shifted(weight_columns(step), step))
+    def traded(value):
+        return lax.ppermute(value, "dp", [(here, here ^ 1) for here in range(senders)])
+
+    def weight_block(row_at, step):
+        column_at = lax.rem(my_group + step, groups) * out_columns
+        return lax.dynamic_slice(out_weight, (row_at, column_at), (half, out_columns))
+
+    weights = {}
+    for step in (1, 3, 2):
+        weights[step] = (shifted(weight_block(first_at, step), step),)
 
     attended = attend(group_ids, arrived, heads_here)
     returned = lax.all_to_all(
@@ -165,14 +281,21 @@
         concat_axis=0,
         tiled=True,
     ).reshape(positions, column_count)
-    mine = jnp.dot(restore, returned, preferred_element_type=jnp.float32).astype(jnp.bfloat16)
-    pieces = [mine]
-    for step in range(1, groups):
-        pieces.append(shifted(mine, step))
-    total = jnp.dot(pieces[0], weights[0], preferred_element_type=jnp.float32)
     for step in (1, 3, 2):
-        total = total + jnp.dot(pieces[step], weights[step], preferred_element_type=jnp.float32)
-    return total.astype(jnp.bfloat16)
+        weights[step] += (traded(weights[step][0]),)
+
+    first, second = restored(first_at, restore, returned)
+    left_first = shifted(first, 1)
+    right_second = shifted(second, -1)
+    left_second = shifted(second, 1)
+    right_first = shifted(first, -1)
+    total = mix((first, second), (weight_block(first_at, 0), weight_block(second_at, 0)))
+    far_first = shifted(left_first, 1)
+    far_second = shifted(right_second, -1)
+    total = mix(
+        (left_first, left_second, right_first, right_second), weights[1] + weights[3], total
+    )
+    return mix((far_first, far_second), weights[2], total, last=True)
 
 
 def solution(mesh):

time: 229 us -> 138 us (0.60)
  waiting for transfers between devices: 162 us -> 68.8 us
  Pallas kernels: 9.11 us -> 23 us
  matrix products: 13.5 us -> 0 us
  starting transfers between devices: 31.7 us -> 34 us
    ppermute x6 -> x9, waiting for transfers between devices: 100 us -> 7.33 us  [shifted(): lax.ppermute(value, 'tensor', [(here, (here + step) % groups) for here in...]
    dot_general x5 -> x0, matrix products: 13.5 us -> none  [the longest x3 9.27 us: local(): jnp.dot(pieces[step], weights[step], preferred_element_type=jnp.float32)]
    pallas_call x0 -> x4, Pallas kernels: none -> 10.7 us  [the longest x3 10.1 us: mix(): pl.pallas_call(functools.partial(mix_kernel, len(rows), total is not None...]
    all_to_all x1, waiting for transfers between devices: 50.4 us -> 39.9 us  [local(): lax.all_to_all(outgoing.reshape(senders, capacity, 3 * column_count), 'dp...]
    all_to_all x1, waiting for transfers between devices: 11.7 us -> 21.6 us  [local(): lax.all_to_all(attended.reshape(senders, capacity, column_count), 'dp', s...]
    pallas_call x1, Pallas kernels: 3.76 us -> 7.83 us  [attend(): pl.pallas_call(functools.partial(attend_kernel, heads), out_shape=jax.Sha...]
    ppermute x6 -> x9, starting transfers between devices: 11.7 us -> 12.6 us  [shifted(): lax.ppermute(value, 'tensor', [(here, (here + step) % groups) for here in...]
  transfers between devices with their start and end apart: 8 -> 14, of which waited for: 5 -> 5; matrix products, arithmetic and copies ran while one was open for 9% -> 8% of each run, Pallas kernels for 0% -> 11%
where the time goes in v2:
time: 138 us; the launch traced here: 137 us
  waiting for transfers between devices  68.8 us (50%)
  starting transfers between devices  34 us (25%)
  Pallas kernels  23 us (17%)
  local copies, waits for them, and re-layouts  10.1 us (7%)
    all_to_all x1, waiting for transfers between devices, local(): lax.all_to_all(outgoing.reshape(senders, capacity, 3 * column_count), 'dp...  39.9 us
    all_to_all x1, waiting for transfers between devices, local(): lax.all_to_all(attended.reshape(senders, capacity, column_count), 'dp', s...  21.6 us
    all_to_all x1, starting transfers between devices, local(): lax.all_to_all(outgoing.reshape(senders, capacity, 3 * column_count), 'dp...  13.1 us
    ppermute x9, starting transfers between devices, shifted(): lax.ppermute(value, 'tensor', [(here, (here + step) % groups) for here in...  12.6 us
    pallas_call x3, Pallas kernels, mix(): pl.pallas_call(functools.partial(mix_kernel, len(rows), total is not None...  10.1 us
    pallas_call x1, Pallas kernels, attend(): pl.pallas_call(functools.partial(attend_kernel, heads), out_shape=jax.Sha...  7.83 us
    ppermute x9, waiting for transfers between devices, shifted(): lax.ppermute(value, 'tensor', [(here, (here + step) % groups) for here in...  7.33 us
    all_to_all x1, starting transfers between devices, local(): lax.all_to_all(attended.reshape(senders, capacity, column_count), 'dp', s...  6.94 us
  transfers between devices with their start and end apart: 14, of which 5 were waited for; matrix products, arithmetic and copies ran while one was open for 8% of the time, Pallas kernels for 11%

profile of v2, /device:TPU:1, one launch (start us, length us, event | category | flops | bytes accessed | tf_op | source)
XLA Modules:
  0.0 137.3 jit_solution(11945706048959388154)
XLA Ops:
  0.0 0.0 copy-start
  0.0 4.5 %pack_rows.1 = (s32[1,384]{1,0:T(1,128)}, bf16[512,2304]{1,0:T(8,128)(2,1)}) custom-call(s32[1,24576]{1,0:T(1,128)} %bitcast.16, bf16[3,384,768]{2,1,0:T(8,128)(2,1)} %bitcast.15), custom_call_target="tpu_custom_call" | custom-call | tf_op jit(solution)/shard_map/pack_rows/pallas_call | solution.py:69
  4.5 13.1 %all-to-all-start = ((bf16[64,8,2304]{2,1,0:T(8,128)(2,1)}), bf16[64,8,2304]{2,1,0:T(8,128)(2,1)}, u32[]{:S(2)}, u32[]{:S(2)}) async-start(bf16[64,8,2304]{2,1,0:T(8,128)(2,1)} %bitcast.14), calls=%async_computation | async-start | bytes 4718592 | tf_op jit(solution)/shard_map/all_to_all | solution.py:240
  17.7 0.0 copy-start.1
  17.8 4.8 %fusion.2 = (bf16[384,1536]{1,0:T(8,128)(2,1)S(1)}, bf16[384,1536]{1,0:T(8,128)(2,1)}, bf16[384,1536]{1,0:T(8,128)(2,1)}, bf16[384,1536]{1,0:T(8,128)(2,1)}, bf16[384,1536]{1,0:T(8,128)(2,1)S(1)}) fusion(bf16[768,6144]{1,0:T(8,128)(2,1)} %param.7, s32[]{:T(128)S(6)} %select_n.73, s32[]{:T(128)S(6)} %select_n.72, s32[]{:T(128)S(6)} %select_n.68, ...), kind=kLoop, calls=%fused_computation.9 | loop fusion | bytes 11796504 | tf_op jit(solution)/shard_map/dynamic_slice | solution.py:270
  22.5 2.7 %collective-permute-start.10 = (bf16[384,1536]{1,0:T(8,128)(2,1)}, bf16[384,1536]{1,0:T(8,128)(2,1)}, u32[]{:S(2)}, u32[]{:S(2)}) collective-permute-start(bf16[384,1536]{1,0:T(8,128)(2,1)} %get-tuple-element.14), channel_id=1, source_target_pairs={{0,3},{1,0},{2,1},{3,2},{4,7},{5,4},{6,5},{7,6},{8,11},{9,8},{10,9... | collective-permute-start | bytes 3538952 | tf_op jit(solution)/shard_map/ppermute | solution.py:261
  25.3 0.0 collective-permute-start.8
  25.3 1.6 %collective-permute-start.4 = (bf16[384,1536]{1,0:T(8,128)(2,1)}, bf16[384,1536]{1,0:T(8,128)(2,1)}, u32[]{:S(2)}, u32[]{:S(2)}) collective-permute-start(bf16[384,1536]{1,0:T(8,128)(2,1)} %get-tuple-element.16), channel_id=1, source_target_pairs={{0,2},{1,3},{2,0},{3,1},{4,6},{5,7},{6,4},{7,5},{8,10},{9,11},{10,... | collective-permute-start | bytes 3538952 | tf_op jit(solution)/shard_map/ppermute | solution.py:261
  26.9 0.0 copy-done.1
  26.9 0.3 fusion.1
  27.2 0.1 reduce_sum.9
  27.3 0.1 copy.6
  27.4 0.1 reduce-window.8
  27.5 0.1 reduce.2
  27.7 0.1 compare_select_fusion
  27.8 0.1 reshape.240
  27.9 0.0 copy-done
  27.9 3.5 %gather_fusion = s32[512]{0:T(512)S(1)} fusion(s32[512]{0:T(512)S(1)} %bitcast.11, s32[1024]{0:T(1024)S(1)} %pad_clamp_fusion), kind=kCustom, calls=%fused_computation | custom fusion | bytes 6144 | tf_op jit(solution)/shard_map/gather | solution.py:254
  31.4 0.1 reshape.239
  31.5 0.1 subtract_select_fusion
  31.6 0.9 select_n.74.group_col_ref
  32.4 0.7 select_n.67.group_row_ref
  33.1 39.9 %all-to-all-done = bf16[64,8,2304]{2,1,0:T(8,128)(2,1)} async-done(((bf16[64,8,2304]{2,1,0:T(8,128)(2,1)}), bf16[64,8,2304]{2,1,0:T(8,128)(2,1)}, u32[]{:S(2)}, u32[]{:S(2)}) %all-to-all-start) | async-done | bytes 2359328 | tf_op jit(solution)/shard_map/all_to_all | solution.py:240
  73.0 7.8 %attend_rows.1 = bf16[512,768]{1,0:T(8,128)(2,1)} custom-call(s32[512,1]{1,0:T(8,128)} %select_n.74.group_col_ref, s32[1,512]{1,0:T(1,128)} %select_n.67.group_row_ref, bf16[512,2304]{1,0:T(8,128)(2,1)} %bitcast.6.data_ref), custom_call_target="tpu_custom_call" | custom-call | tf_op jit(solution)/shard_map/attend_rows/pallas_call | solution.py:138
  80.8 0.0 copy-start.2
  80.8 6.9 %all-to-all-start.1 = ((bf16[64,8,768]{2,1,0:T(8,128)(2,1)}), bf16[64,8,768]{2,1,0:T(8,128)(2,1)S(1)}, u32[]{:S(2)}, u32[]{:S(2)}) async-start(bf16[64,8,768]{2,1,0:T(8,128)(2,1)} %bitcast.13), calls=%async_computation.1 | async-start | bytes 1572864 | tf_op jit(solution)/shard_map/all_to_all | solution.py:277
  87.8 0.0 collective-permute-done.10.refs_6_
  87.8 0.7 collective-permute-start.11
  88.5 0.0 collective-permute-done.8.refs_4_
  88.5 0.1 collective-permute-start.9
  88.6 0.0 collective-permute-done.4.refs_2_
  88.6 0.4 collective-permute-start.5
  89.0 0.0 copy-done.2
  89.1 0.1 fusion.place_ref
  89.2 21.6 %all-to-all-done.1 = bf16[64,8,768]{2,1,0:T(8,128)(2,1)S(1)} async-done(((bf16[64,8,768]{2,1,0:T(8,128)(2,1)}), bf16[64,8,768]{2,1,0:T(8,128)(2,1)S(1)}, u32[]{:S(2)}, u32[]{:S(2)}) %all-to-all-start.1) | async-done | bytes 786464 | tf_op jit(solution)/shard_map/all_to_all | solution.py:277
  110.8 0.6 restore_rows.1
  111.4 1.4 %collective-permute-start = (bf16[384,384]{1,0:T(8,128)(2,1)S(1)}, bf16[384,384]{1,0:T(8,128)(2,1)S(1)}, u32[]{:S(2)}, u32[]{:S(2)}) collective-permute-start(bf16[384,384]{1,0:T(8,128)(2,1)S(1)} %get-tuple-element.11.refs_0_), channel_id=1, source_target_pairs={{0,1},{1,2},{2,3},{3,0},{4,5},{5,6},{6,7},{7,4},{8,9},{9,10},{10,1... | collective-permute-start | bytes 884744 | tf_op jit(solution)/shard_map/ppermute | solution.py:261
  112.7 1.5 %collective-permute-start.2 = (bf16[384,384]{1,0:T(8,128)(2,1)S(1)}, bf16[384,384]{1,0:T(8,128)(2,1)S(1)}, u32[]{:S(2)}, u32[]{:S(2)}) collective-permute-start(bf16[384,384]{1,0:T(8,128)(2,1)S(1)} %get-tuple-element.12.refs_1_), channel_id=1, source_target_pairs={{0,3},{1,0},{2,1},{3,2},{4,7},{5,4},{6,5},{7,6},{8,11},{9,8},{10,9... | collective-permute-start | bytes 884744 | tf_op jit(solution)/shard_map/ppermute | solution.py:261
  114.3 0.0 collective-permute-done.11.refs_7_
  114.3 0.0 collective-permute-start.6
  114.3 0.0 collective-permute-done.9.refs_5_
  114.3 2.7 %collective-permute-start.7 = (bf16[384,384]{1,0:T(8,128)(2,1)S(1)}, bf16[384,384]{1,0:T(8,128)(2,1)S(1)}, u32[]{:S(2)}, u32[]{:S(2)}) collective-permute-start(bf16[384,384]{1,0:T(8,128)(2,1)S(1)} %get-tuple-element.11.refs_0_), channel_id=1, source_target_pairs={{0,3},{1,0},{2,1},{3,2},{4,7},{5,4},{6,5},{7,6},{8,11},{9,8},{10,9... | collective-permute-start | bytes 884744 | tf_op jit(solution)/shard_map/ppermute | solution.py:261
  117.0 3.7 %collective-permute-done.refs_0_ = bf16[384,384]{1,0:T(8,128)(2,1)S(1)} collective-permute-done((bf16[384,384]{1,0:T(8,128)(2,1)S(1)}, bf16[384,384]{1,0:T(8,128)(2,1)S(1)}, u32[]{:S(2)}, u32[]{:S(2)}) %collective-permute-start) | collective-permute-done | bytes 294944 | tf_op jit(solution)/shard_map/ppermute | solution.py:261
  120.7 0.0 collective-permute-start.1
  120.7 0.0 collective-permute-done.2.refs_3_
  120.7 2.7 %collective-permute-start.3 = (bf16[384,384]{1,0:T(8,128)(2,1)S(1)}, bf16[384,384]{1,0:T(8,128)(2,1)S(1)}, u32[]{:S(2)}, u32[]{:S(2)}) collective-permute-start(bf16[384,384]{1,0:T(8,128)(2,1)S(1)} %collective-permute-done.2.refs_3_), channel_id=1, source_target_pairs={{0,3},{1,0},{2,1},{3,2},{4,7},{5,4},{6,5},{7,6},{8,11},{9,8},{10,9... | collective-permute-start | bytes 884744 | tf_op jit(solution)/shard_map/ppermute | solution.py:261
  123.3 1.4 mix_some.2.refs_8_
  124.7 2.3 %collective-permute-done.6.refs_1_ = bf16[384,384]{1,0:T(8,128)(2,1)S(1)} collective-permute-done((bf16[384,384]{1,0:T(8,128)(2,1)S(1)}, bf16[384,384]{1,0:T(8,128)(2,1)S(1)}, u32[]{:S(2)}, u32[]{:S(2)}) %collective-permute-start.6) | collective-permute-done | bytes 294944 | tf_op jit(solution)/shard_map/ppermute | solution.py:261
  127.0 0.0 collective-permute-done.7.refs_2_
  127.0 4.9 %mix_some.3.refs_4_ = f32[384,1536]{1,0:T(8,128)S(1)} custom-call(bf16[384,384]{1,0:T(8,128)(2,1)S(1)} %collective-permute-done.refs_0_, bf16[384,384]{1,0:T(8,128)(2,1)S(1)} %collective-permute-done.6.refs_1_, bf16[384,384]{1,0:T(8,128)(2,1)S(1)} %collective-permute-done.7.refs_2_, bf16[384,384]{1,0:T(8,128)(2,1)S(1)} %collective-permute-done.2.refs_3_, ...), custom_call_target="tpu_custom_call" | custom-call | tf_op jit(solution)/shard_map/mix_some/pallas_call | solution.py:206
  131.9 0.0 collective-permute-done.5.refs_3_
  131.9 1.4 collective-permute-done.1.refs_0_
  133.3 0.0 collective-permute-done.3.refs_1_
  133.3 3.8 %mix_last.1 = bf16[384,1536]{1,0:T(8,128)(2,1)} custom-call(bf16[384,384]{1,0:T(8,128)(2,1)S(1)} %collective-permute-done.1.refs_0_, bf16[384,384]{1,0:T(8,128)(2,1)S(1)} %collective-permute-done.3.refs_1_, bf16[384,1536]{1,0:T(8,128)(2,1)} %collective-permute-done.4.refs_2_, bf16[384,1536]{1,0:T(8,128)(2,1)} %collective-permute-done.5.refs_3_, ...), custom_call_target="tpu_custom_call" | custom-call | tf_op jit(solution)/shard_map/mix_last/pallas_call | solution.py:206
  (4 shorter events, 0.1 us)
Async XLA Ops:
  0.0 27.9 %copy-start = (s32[1,512]{1,0:T(1,128)S(1)}, s32[1,512]{1,0:T(1,128)}, u32[]{:S(2)}) copy-start(s32[1,512]{1,0:T(1,128)} %param.6) | copy-start | bytes 6148
  4.5 68.5 %all-to-all-start = ((bf16[64,8,2304]{2,1,0:T(8,128)(2,1)}), bf16[64,8,2304]{2,1,0:T(8,128)(2,1)}, u32[]{:S(2)}, u32[]{:S(2)}) async-start(bf16[64,8,2304]{2,1,0:T(8,128)(2,1)} %bitcast.14), calls=%async_computation | async-start | bytes 4718592 | tf_op jit(solution)/shard_map/all_to_all | solution.py:240
  17.7 9.2 %copy-start.1 = (s32[24576,1]{0,1:T(1,128)S(1)}, s32[24576,1]{0,1:T(1,128)}, u32[]{:S(2)}) copy-start(s32[24576,1]{0,1:T(1,128)} %param.5) | copy-start | bytes 294916
  22.5 65.3 %collective-permute-start.10 = (bf16[384,1536]{1,0:T(8,128)(2,1)}, bf16[384,1536]{1,0:T(8,128)(2,1)}, u32[]{:S(2)}, u32[]{:S(2)}) collective-permute-start(bf16[384,1536]{1,0:T(8,128)(2,1)} %get-tuple-element.14), channel_id=1, source_target_pairs={{0,3},{1,0},{2,1},{3,2},{4,7},{5,4},{6,5},{7,6},{8,11},{9,8},{10,9... | collective-permute-start | bytes 3538952 | tf_op jit(solution)/shard_map/ppermute | solution.py:261
  25.3 63.3 %collective-permute-start.8 = (bf16[384,1536]{1,0:T(8,128)(2,1)}, bf16[384,1536]{1,0:T(8,128)(2,1)}, u32[]{:S(2)}, u32[]{:S(2)}) collective-permute-start(bf16[384,1536]{1,0:T(8,128)(2,1)} %get-tuple-element.15), channel_id=1, source_target_pairs={{0,1},{1,2},{2,3},{3,0},{4,5},{5,6},{6,7},{7,4},{8,9},{9,10},{10,1... | collective-permute-start | bytes 3538952 | tf_op jit(solution)/shard_map/ppermute | solution.py:261
  25.3 63.4 %collective-permute-start.4 = (bf16[384,1536]{1,0:T(8,128)(2,1)}, bf16[384,1536]{1,0:T(8,128)(2,1)}, u32[]{:S(2)}, u32[]{:S(2)}) collective-permute-start(bf16[384,1536]{1,0:T(8,128)(2,1)} %get-tuple-element.16), channel_id=1, source_target_pairs={{0,2},{1,3},{2,0},{3,1},{4,6},{5,7},{6,4},{7,5},{8,10},{9,11},{10,... | collective-permute-start | bytes 3538952 | tf_op jit(solution)/shard_map/ppermute | solution.py:261
  80.8 8.2 %copy-start.2 = (s32[1,384]{1,0:T(1,128)S(1)}, s32[1,384]{1,0:T(1,128)}, u32[]{:S(2)}) copy-start(s32[1,384]{1,0:T(1,128)} %get-tuple-element.9) | copy-start | bytes 4612
  80.8 29.9 %all-to-all-start.1 = ((bf16[64,8,768]{2,1,0:T(8,128)(2,1)}), bf16[64,8,768]{2,1,0:T(8,128)(2,1)S(1)}, u32[]{:S(2)}, u32[]{:S(2)}) async-start(bf16[64,8,768]{2,1,0:T(8,128)(2,1)} %bitcast.13), calls=%async_computation.1 | async-start | bytes 1572864 | tf_op jit(solution)/shard_map/all_to_all | solution.py:277
  87.8 26.5 %collective-permute-start.11 = (bf16[384,1536]{1,0:T(8,128)(2,1)}, bf16[384,1536]{1,0:T(8,128)(2,1)}, u32[]{:S(2)}, u32[]{:S(2)}) collective-permute-start(bf16[384,1536]{1,0:T(8,128)(2,1)} %collective-permute-done.10.refs_6_), channel_id=1, source_target_pairs={{0,4},{4,0},{8,12},{12,8},{16,20},{20,16},{24,28},{28,24},{32,36},... | collective-permute-start | bytes 3538952 | tf_op jit(solution)/shard_map/ppermute | solution.py:266
  88.5 25.8 %collective-permute-start.9 = (bf16[384,1536]{1,0:T(8,128)(2,1)}, bf16[384,1536]{1,0:T(8,128)(2,1)}, u32[]{:S(2)}, u32[]{:S(2)}) collective-permute-start(bf16[384,1536]{1,0:T(8,128)(2,1)} %collective-permute-done.8.refs_4_), channel_id=1, source_target_pairs={{0,4},{4,0},{8,12},{12,8},{16,20},{20,16},{24,28},{28,24},{32,36},... | collective-permute-start | bytes 3538952 | tf_op jit(solution)/shard_map/ppermute | solution.py:266
  88.6 43.3 %collective-permute-start.5 = (bf16[384,1536]{1,0:T(8,128)(2,1)}, bf16[384,1536]{1,0:T(8,128)(2,1)}, u32[]{:S(2)}, u32[]{:S(2)}) collective-permute-start(bf16[384,1536]{1,0:T(8,128)(2,1)} %collective-permute-done.4.refs_2_), channel_id=1, source_target_pairs={{0,4},{4,0},{8,12},{12,8},{16,20},{20,16},{24,28},{28,24},{32,36},... | collective-permute-start | bytes 3538952 | tf_op jit(solution)/shard_map/ppermute | solution.py:266
  111.4 9.3 %collective-permute-start = (bf16[384,384]{1,0:T(8,128)(2,1)S(1)}, bf16[384,384]{1,0:T(8,128)(2,1)S(1)}, u32[]{:S(2)}, u32[]{:S(2)}) collective-permute-start(bf16[384,384]{1,0:T(8,128)(2,1)S(1)} %get-tuple-element.11.refs_0_), channel_id=1, source_target_pairs={{0,1},{1,2},{2,3},{3,0},{4,5},{5,6},{6,7},{7,4},{8,9},{9,10},{10,1... | collective-permute-start | bytes 884744 | tf_op jit(solution)/shard_map/ppermute | solution.py:261
  112.7 7.9 %collective-permute-start.2 = (bf16[384,384]{1,0:T(8,128)(2,1)S(1)}, bf16[384,384]{1,0:T(8,128)(2,1)S(1)}, u32[]{:S(2)}, u32[]{:S(2)}) collective-permute-start(bf16[384,384]{1,0:T(8,128)(2,1)S(1)} %get-tuple-element.12.refs_1_), channel_id=1, source_target_pairs={{0,3},{1,0},{2,1},{3,2},{4,7},{5,4},{6,5},{7,6},{8,11},{9,8},{10,9... | collective-permute-start | bytes 884744 | tf_op jit(solution)/shard_map/ppermute | solution.py:261
  114.3 12.7 %collective-permute-start.6 = (bf16[384,384]{1,0:T(8,128)(2,1)S(1)}, bf16[384,384]{1,0:T(8,128)(2,1)S(1)}, u32[]{:S(2)}, u32[]{:S(2)}) collective-permute-start(bf16[384,384]{1,0:T(8,128)(2,1)S(1)} %get-tuple-element.12.refs_1_), channel_id=1, source_target_pairs={{0,1},{1,2},{2,3},{3,0},{4,5},{5,6},{6,7},{7,4},{8,9},{9,10},{10,1... | collective-permute-start | bytes 884744 | tf_op jit(solution)/shard_map/ppermute | solution.py:261
  114.3 12.7 %collective-permute-start.7 = (bf16[384,384]{1,0:T(8,128)(2,1)S(1)}, bf16[384,384]{1,0:T(8,128)(2,1)S(1)}, u32[]{:S(2)}, u32[]{:S(2)}) collective-permute-start(bf16[384,384]{1,0:T(8,128)(2,1)S(1)} %get-tuple-element.11.refs_0_), channel_id=1, source_target_pairs={{0,3},{1,0},{2,1},{3,2},{4,7},{5,4},{6,5},{7,6},{8,11},{9,8},{10,9... | collective-permute-start | bytes 884744 | tf_op jit(solution)/shard_map/ppermute | solution.py:261
  120.7 12.6 %collective-permute-start.1 = (bf16[384,384]{1,0:T(8,128)(2,1)S(1)}, bf16[384,384]{1,0:T(8,128)(2,1)S(1)}, u32[]{:S(2)}, u32[]{:S(2)}) collective-permute-start(bf16[384,384]{1,0:T(8,128)(2,1)S(1)} %collective-permute-done.refs_0_), channel_id=1, source_target_pairs={{0,1},{1,2},{2,3},{3,0},{4,5},{5,6},{6,7},{7,4},{8,9},{9,10},{10,1... | collective-permute-start | bytes 884744 | tf_op jit(solution)/shard_map/ppermute | solution.py:261
  120.7 12.6 %collective-permute-start.3 = (bf16[384,384]{1,0:T(8,128)(2,1)S(1)}, bf16[384,384]{1,0:T(8,128)(2,1)S(1)}, u32[]{:S(2)}, u32[]{:S(2)}) collective-permute-start(bf16[384,384]{1,0:T(8,128)(2,1)S(1)} %collective-permute-done.2.refs_3_), channel_id=1, source_target_pairs={{0,3},{1,0},{2,1},{3,2},{4,7},{5,4},{6,5},{7,6},{8,11},{9,8},{10,9... | collective-permute-start | bytes 884744 | tf_op jit(solution)/shard_map/ppermute | solution.py:261
